TPU v7x, 512 devices: a whole 4x8x8 slice. The times are simulated.
512 devices in a mesh: cache: 64 (over x, z, core), rank: 8 (over y).
Axes of the slice: x: 4, y: 8, z: 8, core: 2. Of those that a mesh axis runs over, the one named last changes fastest.
Arguments:
- cand_rows: bfloat16 [64, 64, 4, 1024], P('cache', None, None, 'rank'), may hold values from -48 to 48
- listed: int32 [64], replicated, may hold values from 0 to 63, each once
- hist_len: int32 [64], P('cache'), may hold values from 768 to 3072, as said below
- block_mask: int32 [64, 24], P('cache'), may hold values 0 or 1
- hist_keys: bfloat16 [1, 64, 3072, 1024], P(None, 'cache', None, 'rank'), may hold values from -6 to 6
- hist_values: bfloat16 [1, 64, 3072, 1024], P(None, 'cache', None, 'rank'), may hold values from -6 to 6
- w_query: bfloat16 [1, 1024, 1024], P(None, None, 'rank'), may hold values from -0.1875 to 0.1875
- w_gate: bfloat16 [1, 1024, 1024], P(None, None, 'rank'), may hold values from -0.1875 to 0.1875
- w_out: bfloat16 [1, 1024, 1024], P(None, None, 'rank'), may hold values from -0.1875 to 0.1875
Outputs:
- ranked: bfloat16 [64, 64, 4, 1024], P('cache', None, None, 'rank')
Inputs may be any that keep to these rules, and one draw needn't show every extreme that they name: `hist_len`: some user has exactly 3072 history events. `listed`: each user id appears once.
All inputs are finite; a program needn't handle non-finite values. No bound on the sum of `block_mask` on one device may be relied on, other than what follows from the above.
Results may differ from a plain program's by a relative error of at most 0.0024.
Values may be sent and summed in bfloat16 or wider, within the bound.
A program may use at most 64 MiB of HBM per device.

v0:
```python
import jax
import jax.numpy as jnp
from jax import lax
from jax.sharding import PartitionSpec as P

D = 1024
HEADS = 8
BLOCK = 128
EPSILON = 1e-05
GROUP_BLOCKS = 4


def head_norm(values):
    centre = jnp.mean(values, axis=-1, keepdims=True)
    spread = jnp.mean(jnp.square(values - centre), axis=-1, keepdims=True)
    return (values - centre) * lax.rsqrt(spread + EPSILON)


def attend(queries, key_cache, value_cache, length, block_list, block_live, turn_count):
    head_size = queries.shape[-1]
    score_scale = head_size ** (-0.5)
    within = jnp.arange(BLOCK, dtype=jnp.int32)
    running = jnp.zeros(queries.shape, jnp.float32)

    def one_turn(turn_no, running):
        chosen = lax.dynamic_slice_in_dim(block_list, turn_no * GROUP_BLOCKS, GROUP_BLOCKS)
        chosen_live = lax.dynamic_slice_in_dim(block_live, turn_no * GROUP_BLOCKS, GROUP_BLOCKS)
        key_rows = jnp.take(key_cache, chosen, axis=0).reshape(
            GROUP_BLOCKS * BLOCK, key_cache.shape[2], head_size
        )
        value_rows = jnp.take(value_cache, chosen, axis=0).reshape(
            GROUP_BLOCKS * BLOCK, key_cache.shape[2], head_size
        )
        places = (chosen[:, None] * BLOCK + within[None, :]).reshape(GROUP_BLOCKS * BLOCK)
        live_mask = ((places < length) & jnp.repeat(chosen_live, BLOCK)).astype(jnp.float32)
        scores = (
            jnp.einsum("nkhe,the->nkht", queries, key_rows, preferred_element_type=jnp.float32)
            * score_scale
        )
        weights = (jax.nn.silu(scores) * live_mask).astype(jnp.bfloat16)
        return running + jnp.einsum(
            "nkht,the->nkhe", weights, value_rows, preferred_element_type=jnp.float32
        )

    return lax.fori_loop(0, turn_count, one_turn, running)


def finish(result):
    return lax.all_to_all(result, "cache", split_axis=0, concat_axis=1, tiled=True)


def on_device(
    cand_rows, listed, hist_len, block_mask, hist_keys, hist_values, w_query, w_gate, w_out
):
    head_size = D // HEADS
    local_width = w_query.shape[2]
    local_heads = local_width // head_size
    blocks_total = block_mask.shape[1]
    padded = -(-blocks_total // GROUP_BLOCKS) * GROUP_BLOCKS
    slot_of_user = jnp.argsort(listed)
    outgoing = jnp.take(cand_rows, slot_of_user, axis=1)
    length = hist_len[0]
    starts = jnp.arange(blocks_total, dtype=jnp.int32) * BLOCK
    usable = (block_mask[0] == 1) & (starts < length)
    filler = jnp.zeros((padded - blocks_total,), jnp.int32)
    block_list = jnp.concatenate([jnp.arange(blocks_total, dtype=jnp.int32), filler])
    block_live = jnp.concatenate([usable, filler > 0])
    turn_count = padded // GROUP_BLOCKS
    current = lax.all_to_all(outgoing, "cache", split_axis=1, concat_axis=0, tiled=True)
    whole_rows = lax.all_gather(current, "rank", axis=3, tiled=True)
    normed = head_norm(whole_rows.astype(jnp.float32)).astype(jnp.bfloat16)
    queries = jax.nn.silu(
        jnp.einsum("nukd,de->nuke", normed, w_query[0], preferred_element_type=jnp.float32)
    ).astype(jnp.bfloat16)
    gate_act = jax.nn.silu(
        jnp.einsum("nukd,de->nuke", normed, w_gate[0], preferred_element_type=jnp.float32)
    )
    split_shape = queries.shape[:3] + (local_heads, head_size)
    queries = queries.reshape(split_shape)
    length, block_list, block_live, turn_count = (length, block_list, block_live, turn_count)
    key_cache = hist_keys[0, 0].reshape(blocks_total, BLOCK, local_heads, head_size)
    value_cache = hist_values[0, 0].reshape(blocks_total, BLOCK, local_heads, head_size)
    attended_list = [
        attend(queries[:, 0], key_cache, value_cache, length, block_list, block_live, turn_count)
    ]
    attended = jnp.stack(attended_list, axis=1)
    hidden = (
        (head_norm(attended) * gate_act.reshape(split_shape))
        .reshape(queries.shape[:3] + (local_width,))
        .astype(jnp.bfloat16)
    )
    rows_in = w_out[0]
    projected = jnp.einsum(
        "nukd,de->nuke",
        lax.all_gather(hidden, "rank", axis=3, tiled=True),
        rows_in,
        preferred_element_type=jnp.float32,
    )
    current = (current.astype(jnp.float32) + projected).astype(jnp.bfloat16)
    returned = finish(current)
    return jnp.take(returned, listed, axis=1)


def solution(mesh):
    placed = (
        P("cache", None, None, "rank"),
        P(),
        P("cache"),
        P("cache", None),
        P(None, "cache", None, "rank"),
        P(None, "cache", None, "rank"),
        P(None, None, "rank"),
        P(None, None, "rank"),
        P(None, None, "rank"),
    )
    return jax.shard_map(
        on_device,
        mesh=mesh,
        in_specs=placed,
        out_specs=P("cache", None, None, "rank"),
        check_vma=False,
    )
```

profile of v0, /device:TPU:1, one launch (start us, length us, event | category | flops | bytes accessed | tf_op | source)
XLA Modules:
  0.0 122.2 jit_solution(12769290152046905703)
XLA Ops:
  0.7 2.0 %sort.17 = (s32[64]{0:T(128)}, s32[64]{0:T(128)S(1)}) sort(s32[64]{0:T(128)S(1)} %copy-done.4, s32[64]{0:T(128)S(1)} %iota.13), dimensions={0}, to_apply=%region_0.0 | sort | flops 384 | bytes 1024 | tf_op jit(solution)/shard_map/jit(argsort)/sort | solution.py:60
  2.8 1.5 %gather_fusion.2 = bf16[64,4,128]{2,1,0:T(4,128)(2,1)S(1)} fusion(bf16[64,4,128]{2,1,0:T(4,128)(2,1)} %bitcast.138, s32[1024]{0:T(1024)S(1)} %pad_clamp_fusion.2), kind=kCustom, calls=%fused_computation.clone | custom fusion | bytes 131328 | tf_op jit(solution)/shard_map/jit(_take)/gather | solution.py:61
  4.3 0.8 fusion.45
  5.0 14.8 %all-to-all-start = ((bf16[1,64,4,128]{3,2,0,1:T(4,128)(2,1)}), bf16[1,64,4,128]{3,2,0,1:T(4,128)(2,1)S(1)}, u32[]{:S(2)}, u32[]{:S(2)}) async-start(bf16[1,64,4,128]{3,2,0,1:T(4,128)(2,1)} %fusion.45), calls=%async_computation | async-start | bytes 131072 | tf_op jit(solution)/shard_map/all_to_all | solution.py:69
  21.2 8.5 %all-to-all-done = bf16[1,64,4,128]{3,2,0,1:T(4,128)(2,1)S(1)} async-done(((bf16[1,64,4,128]{3,2,0,1:T(4,128)(2,1)}), bf16[1,64,4,128]{3,2,0,1:T(4,128)(2,1)S(1)}, u32[]{:S(2)}, u32[]{:S(2)}) %all-to-all-start) | async-done | bytes 65568 | tf_op jit(solution)/shard_map/all_to_all | solution.py:69
  29.7 15.8 %all-gather = bf16[1,64,4,1024]{3,2,0,1:T(4,128)(2,1)S(1)} all-gather(bf16[1,64,4,128]{3,2,0,1:T(4,128)(2,1)S(1)} %all-to-all-done), channel_id=2, replica_groups=mesh['cache'=64,'rank'=8] {'rank'}, dimensions={3}, use_global_device_ids=true | all-gather | bytes 589824 | tf_op jit(solution)/shard_map/all_gather | solution.py:70
  47.0 29.7 %while.14 = (s32[]{:T(128)}, f32[64,4,1,128]{3,0,1,2:T(8,128)S(1)}, s32[24]{0:T(128)S(1)}, bf16[24,128,1,128]{3,1,0,2:T(8,128)(2,1)}, bf16[24,128,1,128]{3,1,0,2...) while((s32[]{:T(128)}, f32[64,4,1,128]{3,0,1,2:T(8,128)S(1)}, ...), condition=%wide.region_4.7_spmd.clone, body=%wide.region_3.6_spmd.clone.sunk | while | flops 68226080 | bytes 1646929 | solution.py:45
  47.1 1.7 %gather_fusion = bf16[4,128,128]{2,1,0:T(8,128)(2,1)S(1)} fusion(bf16[24,128,128]{2,1,0:T(8,128)(2,1)} %bitcast.136, s32[1024]{0:T(1024)S(1)} %pad_clamp_fusion.4), kind=kCustom, calls=%fused_computation.3.clone.clone.1 | custom fusion | bytes 262160 | tf_op jit(solution)/shard_map/while/body/eval_jaxpr/jit(_take)/gather | solution.py:28
  48.8 1.7 %gather_fusion.1 = bf16[4,128,128]{2,1,0:T(8,128)(2,1)S(1)} fusion(bf16[24,128,128]{2,1,0:T(8,128)(2,1)} %bitcast.134, s32[1024]{0:T(1024)S(1)} %pad_clamp_fusion.4), kind=kCustom, calls=%fused_computation.1.clone.clone.1 | custom fusion | bytes 262160 | tf_op jit(solution)/shard_map/while/body/eval_jaxpr/jit(_take)/gather | solution.py:31
  50.8 0.7 convert_bitcast_fusion.3
  52.0 1.7 %gather_fusion = bf16[4,128,128]{2,1,0:T(8,128)(2,1)S(1)} fusion(bf16[24,128,128]{2,1,0:T(8,128)(2,1)} %bitcast.136, s32[1024]{0:T(1024)S(1)} %pad_clamp_fusion.4), kind=kCustom, calls=%fused_computation.3.clone.clone.1 | custom fusion | bytes 262160 | tf_op jit(solution)/shard_map/while/body/eval_jaxpr/jit(_take)/gather | solution.py:28
  53.7 1.7 %gather_fusion.1 = bf16[4,128,128]{2,1,0:T(8,128)(2,1)S(1)} fusion(bf16[24,128,128]{2,1,0:T(8,128)(2,1)} %bitcast.134, s32[1024]{0:T(1024)S(1)} %pad_clamp_fusion.4), kind=kCustom, calls=%fused_computation.1.clone.clone.1 | custom fusion | bytes 262160 | tf_op jit(solution)/shard_map/while/body/eval_jaxpr/jit(_take)/gather | solution.py:31
  57.0 1.7 %gather_fusion = bf16[4,128,128]{2,1,0:T(8,128)(2,1)S(1)} fusion(bf16[24,128,128]{2,1,0:T(8,128)(2,1)} %bitcast.136, s32[1024]{0:T(1024)S(1)} %pad_clamp_fusion.4), kind=kCustom, calls=%fused_computation.3.clone.clone.1 | custom fusion | bytes 262160 | tf_op jit(solution)/shard_map/while/body/eval_jaxpr/jit(_take)/gather | solution.py:28
  58.7 1.7 %gather_fusion.1 = bf16[4,128,128]{2,1,0:T(8,128)(2,1)S(1)} fusion(bf16[24,128,128]{2,1,0:T(8,128)(2,1)} %bitcast.134, s32[1024]{0:T(1024)S(1)} %pad_clamp_fusion.4), kind=kCustom, calls=%fused_computation.1.clone.clone.1 | custom fusion | bytes 262160 | tf_op jit(solution)/shard_map/while/body/eval_jaxpr/jit(_take)/gather | solution.py:31
  61.9 1.7 %gather_fusion = bf16[4,128,128]{2,1,0:T(8,128)(2,1)S(1)} fusion(bf16[24,128,128]{2,1,0:T(8,128)(2,1)} %bitcast.136, s32[1024]{0:T(1024)S(1)} %pad_clamp_fusion.4), kind=kCustom, calls=%fused_computation.3.clone.clone.1 | custom fusion | bytes 262160 | tf_op jit(solution)/shard_map/while/body/eval_jaxpr/jit(_take)/gather | solution.py:28
  63.6 1.7 %gather_fusion.1 = bf16[4,128,128]{2,1,0:T(8,128)(2,1)S(1)} fusion(bf16[24,128,128]{2,1,0:T(8,128)(2,1)} %bitcast.134, s32[1024]{0:T(1024)S(1)} %pad_clamp_fusion.4), kind=kCustom, calls=%fused_computation.1.clone.clone.1 | custom fusion | bytes 262160 | tf_op jit(solution)/shard_map/while/body/eval_jaxpr/jit(_take)/gather | solution.py:31
  66.9 1.7 %gather_fusion = bf16[4,128,128]{2,1,0:T(8,128)(2,1)S(1)} fusion(bf16[24,128,128]{2,1,0:T(8,128)(2,1)} %bitcast.136, s32[1024]{0:T(1024)S(1)} %pad_clamp_fusion.4), kind=kCustom, calls=%fused_computation.3.clone.clone.1 | custom fusion | bytes 262160 | tf_op jit(solution)/shard_map/while/body/eval_jaxpr/jit(_take)/gather | solution.py:28
  68.6 1.7 %gather_fusion.1 = bf16[4,128,128]{2,1,0:T(8,128)(2,1)S(1)} fusion(bf16[24,128,128]{2,1,0:T(8,128)(2,1)} %bitcast.134, s32[1024]{0:T(1024)S(1)} %pad_clamp_fusion.4), kind=kCustom, calls=%fused_computation.1.clone.clone.1 | custom fusion | bytes 262160 | tf_op jit(solution)/shard_map/while/body/eval_jaxpr/jit(_take)/gather | solution.py:31
  71.8 1.7 %gather_fusion = bf16[4,128,128]{2,1,0:T(8,128)(2,1)S(1)} fusion(bf16[24,128,128]{2,1,0:T(8,128)(2,1)} %bitcast.136, s32[1024]{0:T(1024)S(1)} %pad_clamp_fusion.4), kind=kCustom, calls=%fused_computation.3.clone.clone.1 | custom fusion | bytes 262160 | tf_op jit(solution)/shard_map/while/body/eval_jaxpr/jit(_take)/gather | solution.py:28
  73.6 1.7 %gather_fusion.1 = bf16[4,128,128]{2,1,0:T(8,128)(2,1)S(1)} fusion(bf16[24,128,128]{2,1,0:T(8,128)(2,1)} %bitcast.134, s32[1024]{0:T(1024)S(1)} %pad_clamp_fusion.4), kind=kCustom, calls=%fused_computation.1.clone.clone.1 | custom fusion | bytes 262160 | tf_op jit(solution)/shard_map/while/body/eval_jaxpr/jit(_take)/gather | solution.py:31
  78.0 19.5 %all-gather.1 = bf16[64,4,1024]{2,0,1:T(8,128)(2,1)S(1)} all-gather(bf16[64,4,128]{2,0,1:T(8,128)(2,1)S(1)} %fusion.31), channel_id=3, replica_groups=mesh['cache'=64,'rank'=8] {'rank'}, dimensions={2}, use_global_device_ids=true | all-gather | bytes 589824 | tf_op jit(solution)/shard_map/all_gather | solution.py:95
  98.5 12.4 %all-to-all-start.1 = ((bf16[64,1,4,128]{3,2,1,0:T(4,128)(2,1)}), bf16[64,1,4,128]{3,2,1,0:T(4,128)(2,1)S(1)}, u32[]{:S(2)}, u32[]{:S(2)}) async-start(bf16[64,1,4,128]{3,2,1,0:T(4,128)(2,1)} %copy.46), calls=%async_computation.1 | async-start | bytes 131072 | tf_op jit(solution)/shard_map/all_to_all | solution.py:49
  110.9 9.9 %all-to-all-done.1 = bf16[64,1,4,128]{3,2,1,0:T(4,128)(2,1)S(1)} async-done(((bf16[64,1,4,128]{3,2,1,0:T(4,128)(2,1)}), bf16[64,1,4,128]{3,2,1,0:T(4,128)(2,1)S(1)}, u32[]{:S(2)}, u32[]{:S(2)}) %all-to-all-start.1) | async-done | bytes 65568 | tf_op jit(solution)/shard_map/all_to_all | solution.py:49
  121.4 0.8 bitcast_select_fusion.2
  (75 shorter events, 14.0 us)
Async XLA Ops:
  0.0 46.6 %copy-start = (bf16[1,1024,128]{2,1,0:T(8,128)(2,1)S(1)}, bf16[1,1024,128]{2,1,0:T(8,128)(2,1)}, u32[]{:S(2)}) copy-start(bf16[1,1024,128]{2,1,0:T(8,128)(2,1)} %param.21) | copy-start | bytes 786436
  0.0 0.7 copy-start.4
  5.0 24.6 %all-to-all-start = ((bf16[1,64,4,128]{3,2,0,1:T(4,128)(2,1)}), bf16[1,64,4,128]{3,2,0,1:T(4,128)(2,1)S(1)}, u32[]{:S(2)}, u32[]{:S(2)}) async-start(bf16[1,64,4,128]{3,2,0,1:T(4,128)(2,1)} %fusion.45), calls=%async_computation | async-start | bytes 131072 | tf_op jit(solution)/shard_map/all_to_all | solution.py:69
  20.5 0.7 copy-start.3
  76.7 1.0 copy-start.2
  78.0 19.5 %copy-start.1 = (bf16[1,1024,128]{2,1,0:T(8,128)(2,1)S(1)}, bf16[1,1024,128]{2,1,0:T(8,128)(2,1)}, u32[]{:S(2)}) copy-start(bf16[1,1024,128]{2,1,0:T(8,128)(2,1)} %param.23) | copy-start | bytes 786436
  98.5 22.3 %all-to-all-start.1 = ((bf16[64,1,4,128]{3,2,1,0:T(4,128)(2,1)}), bf16[64,1,4,128]{3,2,1,0:T(4,128)(2,1)S(1)}, u32[]{:S(2)}, u32[]{:S(2)}) async-start(bf16[64,1,4,128]{3,2,1,0:T(4,128)(2,1)} %copy.46), calls=%async_computation.1 | async-start | bytes 131072 | tf_op jit(solution)/shard_map/all_to_all | solution.py:49
where the time goes:
time: 123 us; the launch traced here: 122 us
  blocking collectives  35.3 us (29%)
  starting transfers between devices  27.3 us (22%)
  local copies, waits for them, and re-layouts  25.8 us (21%)
  waiting for transfers between devices  18.3 us (15%)
  other arithmetic  10.9 us (9%)
  matrix products  3.56 us (3%)
    all_gather x1, blocking collectives, on_device(): lax.all_gather(hidden, 'rank', axis=3, tiled=True)  19.5 us
    all_gather x1, blocking collectives, on_device(): whole_rows = lax.all_gather(current, 'rank', axis=3, tiled=True)  15.8 us
    all_to_all x1, starting transfers between devices, on_device(): lax.all_to_all(outgoing, 'cache', split_axis=1, concat_axis=0, tiled=True)  14.8 us
    all_to_all x1, starting transfers between devices, finish(): lax.all_to_all(result, 'cache', split_axis=0, concat_axis=1, tiled=True)  12.4 us
    gather x6, local copies, waits for them, and re-layouts, one_turn(): jnp.take(key_cache, chosen, axis=0)  10.2 us
    gather x6, local copies, waits for them, and re-layouts, one_turn(): jnp.take(value_cache, chosen, axis=0)  10.2 us
    all_to_all x1, waiting for transfers between devices, finish(): lax.all_to_all(result, 'cache', split_axis=0, concat_axis=1, tiled=True)  9.87 us
    all_to_all x1, waiting for transfers between devices, on_device(): lax.all_to_all(outgoing, 'cache', split_axis=1, concat_axis=0, tiled=True)  8.45 us
  transfers between devices with their start and end apart: 2, of which 2 were waited for; matrix products, arithmetic and copies ran while one was open for 0% of the time, Pallas kernels for 0%

commit v1 on v0

--- a/solution.py
+++ b/solution.py
@@ -90,12 +90,50 @@
         .astype(jnp.bfloat16)
     )
     rows_in = w_out[0]
+    piece_out = lax.axis_size("rank")
+    carry = lax.axis_index("rank")
+    finding, w2, before = (piece_out, carry, hidden.shape[3])
+    by_place = []
+    at = 0
+    while at < finding:
+        by_place.append((at, (at + 1) % finding))
+        at += 1
+    runs = []
+    at = 0
+    while at < finding:
+        runs.append((at, (at - 1) % finding))
+        at = at + 1
+    f_next = finding // 2
+    near = x_now = hidden
     projected = jnp.einsum(
         "nukd,de->nuke",
-        lax.all_gather(hidden, "rank", axis=3, tiled=True),
-        rows_in,
+        hidden,
+        lax.dynamic_slice_in_dim(rows_in, w2 * before, hidden.shape[3], axis=0),
         preferred_element_type=jnp.float32,
     )
+    to_i = 1
+    while to_i < f_next + 1:
+        near = lax.ppermute(near, axis_name="rank", perm=by_place)
+        if to_i < finding - f_next:
+            x_now = lax.ppermute(x_now, "rank", runs)
+            block_last = jnp.einsum(
+                "nukd,de->nuke",
+                x_now,
+                lax.dynamic_slice_in_dim(
+                    rows_in, (w2 + to_i) % finding * before, x_now.shape[3], axis=0
+                ),
+                preferred_element_type=jnp.float32,
+            )
+            projected = projected + block_last
+        projected = projected + jnp.einsum(
+            "nukd,de->nuke",
+            near,
+            lax.dynamic_slice_in_dim(
+                rows_in, (w2 - to_i) % finding * before, near.shape[3], axis=0
+            ),
+            preferred_element_type=jnp.float32,
+        )
+        to_i = to_i + 1
     current = (current.astype(jnp.float32) + projected).astype(jnp.bfloat16)
     returned = finish(current)
     return jnp.take(returned, listed, axis=1)

time: 123 us -> 130 us (1.057)
  starting transfers between devices: 27.3 us -> 47.3 us
  blocking collectives: 35.3 us -> 15.8 us
  waiting for transfers between devices: 18.3 us -> 22.1 us
    ppermute x0 -> x7, starting transfers between devices: none -> 21.4 us  [the longest x3 13.2 us: on_device(): x_now = lax.ppermute(x_now, 'rank', runs)]
    all_gather x1 -> x0, blocking collectives: 19.5 us -> none  [on_device(): lax.all_gather(hidden, 'rank', axis=3, tiled=True)]
    ppermute x0 -> x7, waiting for transfers between devices: none -> 3.98 us  [the longest x4 3.97 us: on_device(): near = lax.ppermute(near, axis_name='rank', perm=by_place)]
    all_to_all x1, starting transfers between devices: 12.4 us -> 11.1 us  [finish(): lax.all_to_all(result, 'cache', split_axis=0, concat_axis=1, tiled=True)]
  transfers between devices with their start and end apart: 2 -> 9, of which waited for: 2 -> 3; matrix products, arithmetic and copies ran while one was open for 0% -> 1% of each run, Pallas kernels for 0% -> 0%
where the time goes in v1:
time: 130 us; the launch traced here: 128 us
  starting transfers between devices  47.3 us (36%)
  local copies, waits for them, and re-layouts  26.3 us (20%)
  waiting for transfers between devices  22.1 us (17%)
  blocking collectives  15.8 us (12%)
  other arithmetic  10.9 us (8%)
  matrix products  4.47 us (3%)
    all_gather x1, blocking collectives, on_device(): whole_rows = lax.all_gather(current, 'rank', axis=3, tiled=True)  15.8 us
    all_to_all x1, starting transfers between devices, on_device(): lax.all_to_all(outgoing, 'cache', split_axis=1, concat_axis=0, tiled=True)  14.8 us
    ppermute x3, starting transfers between devices, on_device(): x_now = lax.ppermute(x_now, 'rank', runs)  13.2 us
    all_to_all x1, starting transfers between devices, finish(): lax.all_to_all(result, 'cache', split_axis=0, concat_axis=1, tiled=True)  11.1 us
    gather x6, local copies, waits for them, and re-layouts, one_turn(): jnp.take(key_cache, chosen, axis=0)  10.2 us
    gather x6, local copies, waits for them, and re-layouts, one_turn(): jnp.take(value_cache, chosen, axis=0)  10.2 us
    all_to_all x1, waiting for transfers between devices, finish(): lax.all_to_all(result, 'cache', split_axis=0, concat_axis=1, tiled=True)  9.87 us
    all_to_all x1, waiting for transfers between devices, on_device(): lax.all_to_all(outgoing, 'cache', split_axis=1, concat_axis=0, tiled=True)  8.3 us
  transfers between devices with their start and end apart: 9, of which 3 were waited for; matrix products, arithmetic and copies ran while one was open for 1% of the time, Pallas kernels for 0%

profile of v1, /device:TPU:1, one launch (start us, length us, event | category | flops | bytes accessed | tf_op | source)
XLA Modules:
  0.0 128.5 jit_solution(4080672387346761620)
XLA Ops:
  0.7 2.0 %sort.17 = (s32[64]{0:T(128)}, s32[64]{0:T(128)S(1)}) sort(s32[64]{0:T(128)S(1)} %copy-done.4, s32[64]{0:T(128)S(1)} %iota.13), dimensions={0}, to_apply=%region_0.0 | sort | flops 384 | bytes 1024 | tf_op jit(solution)/shard_map/jit(argsort)/sort | solution.py:60
  5.0 14.8 %all-to-all-start = ((bf16[1,64,4,128]{3,2,0,1:T(4,128)(2,1)}), bf16[1,64,4,128]{3,2,0,1:T(4,128)(2,1)S(1)}, u32[]{:S(2)}, u32[]{:S(2)}) async-start(bf16[1,64,4,128]{3,2,0,1:T(4,128)(2,1)} %fusion.56), calls=%async_computation | async-start | bytes 131072 | tf_op jit(solution)/shard_map/all_to_all | solution.py:69
  21.4 8.3 %all-to-all-done = bf16[1,64,4,128]{3,2,0,1:T(4,128)(2,1)S(1)} async-done(((bf16[1,64,4,128]{3,2,0,1:T(4,128)(2,1)}), bf16[1,64,4,128]{3,2,0,1:T(4,128)(2,1)S(1)}, u32[]{:S(2)}, u32[]{:S(2)}) %all-to-all-start) | async-done | bytes 65568 | tf_op jit(solution)/shard_map/all_to_all | solution.py:69
  29.7 15.8 %all-gather = bf16[1,64,4,1024]{3,2,0,1:T(4,128)(2,1)S(1)} all-gather(bf16[1,64,4,128]{3,2,0,1:T(4,128)(2,1)S(1)} %all-to-all-done), channel_id=2, replica_groups=mesh['cache'=64,'rank'=8] {'rank'}, dimensions={3}, use_global_device_ids=true | all-gather | bytes 589824 | tf_op jit(solution)/shard_map/all_gather | solution.py:70
  47.6 29.7 %while.14 = (s32[]{:T(128)}, f32[64,4,1,128]{3,0,1,2:T(8,128)S(1)}, s32[24]{0:T(128)S(1)}, bf16[24,128,1,128]{3,1,0,2:T(8,128)(2,1)}, bf16[24,128,1,128]{3,1,0,2...) while((s32[]{:T(128)}, f32[64,4,1,128]{3,0,1,2:T(8,128)S(1)}, ...), condition=%wide.region_4.7_spmd.clone, body=%wide.region_3.6_spmd.clone.sunk | while | flops 68226080 | bytes 1646937 | solution.py:45
  47.7 1.7 %gather_fusion = bf16[4,128,128]{2,1,0:T(8,128)(2,1)S(1)} fusion(bf16[24,128,128]{2,1,0:T(8,128)(2,1)} %bitcast.186, s32[1024]{0:T(1024)S(1)} %pad_clamp_fusion.4), kind=kCustom, calls=%fused_computation.3.clone.clone.1 | custom fusion | bytes 262160 | tf_op jit(solution)/shard_map/while/body/eval_jaxpr/jit(_take)/gather | solution.py:28
  49.4 1.7 %gather_fusion.1 = bf16[4,128,128]{2,1,0:T(8,128)(2,1)S(1)} fusion(bf16[24,128,128]{2,1,0:T(8,128)(2,1)} %bitcast.184, s32[1024]{0:T(1024)S(1)} %pad_clamp_fusion.4), kind=kCustom, calls=%fused_computation.1.clone.clone.1 | custom fusion | bytes 262160 | tf_op jit(solution)/shard_map/while/body/eval_jaxpr/jit(_take)/gather | solution.py:31
  52.6 1.7 %gather_fusion = bf16[4,128,128]{2,1,0:T(8,128)(2,1)S(1)} fusion(bf16[24,128,128]{2,1,0:T(8,128)(2,1)} %bitcast.186, s32[1024]{0:T(1024)S(1)} %pad_clamp_fusion.4), kind=kCustom, calls=%fused_computation.3.clone.clone.1 | custom fusion | bytes 262160 | tf_op jit(solution)/shard_map/while/body/eval_jaxpr/jit(_take)/gather | solution.py:28
  57.6 1.7 %gather_fusion = bf16[4,128,128]{2,1,0:T(8,128)(2,1)S(1)} fusion(bf16[24,128,128]{2,1,0:T(8,128)(2,1)} %bitcast.186, s32[1024]{0:T(1024)S(1)} %pad_clamp_fusion.4), kind=kCustom, calls=%fused_computation.3.clone.clone.1 | custom fusion | bytes 262160 | tf_op jit(solution)/shard_map/while/body/eval_jaxpr/jit(_take)/gather | solution.py:28
  59.3 1.7 %gather_fusion.1 = bf16[4,128,128]{2,1,0:T(8,128)(2,1)S(1)} fusion(bf16[24,128,128]{2,1,0:T(8,128)(2,1)} %bitcast.184, s32[1024]{0:T(1024)S(1)} %pad_clamp_fusion.4), kind=kCustom, calls=%fused_computation.1.clone.clone.1 | custom fusion | bytes 262160 | tf_op jit(solution)/shard_map/while/body/eval_jaxpr/jit(_take)/gather | solution.py:31
  62.5 1.7 %gather_fusion = bf16[4,128,128]{2,1,0:T(8,128)(2,1)S(1)} fusion(bf16[24,128,128]{2,1,0:T(8,128)(2,1)} %bitcast.186, s32[1024]{0:T(1024)S(1)} %pad_clamp_fusion.4), kind=kCustom, calls=%fused_computation.3.clone.clone.1 | custom fusion | bytes 262160 | tf_op jit(solution)/shard_map/while/body/eval_jaxpr/jit(_take)/gather | solution.py:28
  64.2 1.7 %gather_fusion.1 = bf16[4,128,128]{2,1,0:T(8,128)(2,1)S(1)} fusion(bf16[24,128,128]{2,1,0:T(8,128)(2,1)} %bitcast.184, s32[1024]{0:T(1024)S(1)} %pad_clamp_fusion.4), kind=kCustom, calls=%fused_computation.1.clone.clone.1 | custom fusion | bytes 262160 | tf_op jit(solution)/shard_map/while/body/eval_jaxpr/jit(_take)/gather | solution.py:31
  67.5 1.7 %gather_fusion = bf16[4,128,128]{2,1,0:T(8,128)(2,1)S(1)} fusion(bf16[24,128,128]{2,1,0:T(8,128)(2,1)} %bitcast.186, s32[1024]{0:T(1024)S(1)} %pad_clamp_fusion.4), kind=kCustom, calls=%fused_computation.3.clone.clone.1 | custom fusion | bytes 262160 | tf_op jit(solution)/shard_map/while/body/eval_jaxpr/jit(_take)/gather | solution.py:28
  69.2 1.7 %gather_fusion.1 = bf16[4,128,128]{2,1,0:T(8,128)(2,1)S(1)} fusion(bf16[24,128,128]{2,1,0:T(8,128)(2,1)} %bitcast.184, s32[1024]{0:T(1024)S(1)} %pad_clamp_fusion.4), kind=kCustom, calls=%fused_computation.1.clone.clone.1 | custom fusion | bytes 262160 | tf_op jit(solution)/shard_map/while/body/eval_jaxpr/jit(_take)/gather | solution.py:31
  78.6 2.5 %collective-permute-start.1 = (bf16[64,1,4,128]{3,0,2,1:T(8,128)(2,1)S(1)}, bf16[64,1,4,128]{3,0,2,1:T(8,128)(2,1)S(1)}, u32[]{:S(2)}, u32[]{:S(2)}) collective-permute-start(bf16[64,1,4,128]{3,0,2,1:T(8,128)(2,1)S(1)} %bitcast.188), channel_id=1, source_target_pairs={{0,1},{1,2},{2,3},{3,4},{4,5},{5,6},{6,7},{7,0},{8,9},{9,10},{10,1... | collective-permute-start | bytes 196616 | tf_op jit(solution)/shard_map/ppermute | solution.py:116
  81.0 4.0 %collective-permute-start = (bf16[64,1,4,128]{3,0,2,1:T(8,128)(2,1)S(1)}, bf16[64,1,4,128]{3,0,2,1:T(8,128)(2,1)S(1)}, u32[]{:S(2)}, u32[]{:S(2)}) collective-permute-start(bf16[64,1,4,128]{3,0,2,1:T(8,128)(2,1)S(1)} %bitcast.189), channel_id=1, source_target_pairs={{0,7},{1,0},{2,1},{3,2},{4,3},{5,4},{6,5},{7,6},{8,15},{9,8},{10,9... | collective-permute-start | bytes 196616 | tf_op jit(solution)/shard_map/ppermute | solution.py:118
  85.2 1.9 %collective-permute-start.3 = (bf16[64,1,4,128]{3,0,2,1:T(8,128)(2,1)S(1)}, bf16[64,1,4,128]{3,0,2,1:T(8,128)(2,1)S(1)}, u32[]{:S(2)}, u32[]{:S(2)}) collective-permute-start(bf16[64,1,4,128]{3,0,2,1:T(8,128)(2,1)S(1)} %collective-permute-done.1), channel_id=1, source_target_pairs={{0,1},{1,2},{2,3},{3,4},{4,5},{5,6},{6,7},{7,0},{8,9},{9,10},{10,1... | collective-permute-start | bytes 196616 | tf_op jit(solution)/shard_map/ppermute | solution.py:116
  87.2 4.6 %collective-permute-start.2 = (bf16[64,1,4,128]{3,0,2,1:T(8,128)(2,1)S(1)}, bf16[64,1,4,128]{3,0,2,1:T(8,128)(2,1)S(1)}, u32[]{:S(2)}, u32[]{:S(2)}) collective-permute-start(bf16[64,1,4,128]{3,0,2,1:T(8,128)(2,1)S(1)} %collective-permute-done), channel_id=1, source_target_pairs={{0,7},{1,0},{2,1},{3,2},{4,3},{5,4},{6,5},{7,6},{8,15},{9,8},{10,9... | collective-permute-start | bytes 196616 | tf_op jit(solution)/shard_map/ppermute | solution.py:118
  92.1 1.9 %collective-permute-start.5 = (bf16[64,1,4,128]{3,0,2,1:T(8,128)(2,1)S(1)}, bf16[64,1,4,128]{3,0,2,1:T(8,128)(2,1)S(1)}, u32[]{:S(2)}, u32[]{:S(2)}) collective-permute-start(bf16[64,1,4,128]{3,0,2,1:T(8,128)(2,1)S(1)} %collective-permute-done.3), channel_id=1, source_target_pairs={{0,1},{1,2},{2,3},{3,4},{4,5},{5,6},{6,7},{7,0},{8,9},{9,10},{10,1... | collective-permute-start | bytes 196616 | tf_op jit(solution)/shard_map/ppermute | solution.py:116
  94.2 4.6 %collective-permute-start.4 = (bf16[64,1,4,128]{3,0,2,1:T(8,128)(2,1)S(1)}, bf16[64,1,4,128]{3,0,2,1:T(8,128)(2,1)S(1)}, u32[]{:S(2)}, u32[]{:S(2)}) collective-permute-start(bf16[64,1,4,128]{3,0,2,1:T(8,128)(2,1)S(1)} %collective-permute-done.2), channel_id=1, source_target_pairs={{0,7},{1,0},{2,1},{3,2},{4,3},{5,4},{6,5},{7,6},{8,15},{9,8},{10,9... | collective-permute-start | bytes 196616 | tf_op jit(solution)/shard_map/ppermute | solution.py:118
  98.9 1.9 %collective-permute-start.6 = (bf16[64,1,4,128]{3,0,2,1:T(8,128)(2,1)S(1)}, bf16[64,1,4,128]{3,0,2,1:T(8,128)(2,1)S(1)}, u32[]{:S(2)}, u32[]{:S(2)}) collective-permute-start(bf16[64,1,4,128]{3,0,2,1:T(8,128)(2,1)S(1)} %collective-permute-done.5), channel_id=1, source_target_pairs={{0,1},{1,2},{2,3},{3,4},{4,5},{5,6},{6,7},{7,0},{8,9},{9,10},{10,1... | collective-permute-start | bytes 196616 | tf_op jit(solution)/shard_map/ppermute | solution.py:116
  101.2 4.0 %collective-permute-done.6 = bf16[64,1,4,128]{3,0,2,1:T(8,128)(2,1)S(1)} collective-permute-done((bf16[64,1,4,128]{3,0,2,1:T(8,128)(2,1)S(1)}, bf16[64,1,4,128]{3,0,2,1:T(8,128)(2,1)S(1)}, u32[]{:S(2)}, u32[]{:S(2)}) %collective-permute-start.6) | collective-permute-done | bytes 65568 | tf_op jit(solution)/shard_map/ppermute | solution.py:116
  106.0 11.1 %all-to-all-start.1 = ((bf16[64,1,4,128]{3,2,1,0:T(4,128)(2,1)}), bf16[64,1,4,128]{3,2,1,0:T(4,128)(2,1)S(1)}, u32[]{:S(2)}, u32[]{:S(2)}) async-start(bf16[64,1,4,128]{3,2,1,0:T(4,128)(2,1)} %copy.46), calls=%async_computation.1 | async-start | bytes 131072 | tf_op jit(solution)/shard_map/all_to_all | solution.py:49
  117.2 9.9 %all-to-all-done.1 = bf16[64,1,4,128]{3,2,1,0:T(4,128)(2,1)S(1)} async-done(((bf16[64,1,4,128]{3,2,1,0:T(4,128)(2,1)}), bf16[64,1,4,128]{3,2,1,0:T(4,128)(2,1)S(1)}, u32[]{:S(2)}, u32[]{:S(2)}) %all-to-all-start.1) | async-done | bytes 65568 | tf_op jit(solution)/shard_map/all_to_all | solution.py:49
  (95 shorter events, 24.3 us)
Async XLA Ops:
  0.0 85.1 %copy-start = (bf16[1,1024,128]{2,1,0:T(8,128)(2,1)S(1)}, bf16[1,1024,128]{2,1,0:T(8,128)(2,1)}, u32[]{:S(2)}) copy-start(bf16[1,1024,128]{2,1,0:T(8,128)(2,1)} %param.23) | copy-start | bytes 786436
  0.0 0.7 copy-start.4
  5.0 24.6 %all-to-all-start = ((bf16[1,64,4,128]{3,2,0,1:T(4,128)(2,1)}), bf16[1,64,4,128]{3,2,0,1:T(4,128)(2,1)S(1)}, u32[]{:S(2)}, u32[]{:S(2)}) async-start(bf16[1,64,4,128]{3,2,0,1:T(4,128)(2,1)} %fusion.56), calls=%async_computation | async-start | bytes 131072 | tf_op jit(solution)/shard_map/all_to_all | solution.py:69
  20.7 0.7 copy-start.3
  46.3 1.0 copy-start.1
  77.3 1.0 copy-start.2
  78.6 6.7 %collective-permute-start.1 = (bf16[64,1,4,128]{3,0,2,1:T(8,128)(2,1)S(1)}, bf16[64,1,4,128]{3,0,2,1:T(8,128)(2,1)S(1)}, u32[]{:S(2)}, u32[]{:S(2)}) collective-permute-start(bf16[64,1,4,128]{3,0,2,1:T(8,128)(2,1)S(1)} %bitcast.188), channel_id=1, source_target_pairs={{0,1},{1,2},{2,3},{3,4},{4,5},{5,6},{6,7},{7,0},{8,9},{9,10},{10,1... | collective-permute-start | bytes 196616 | tf_op jit(solution)/shard_map/ppermute | solution.py:116
  81.0 6.1 %collective-permute-start = (bf16[64,1,4,128]{3,0,2,1:T(8,128)(2,1)S(1)}, bf16[64,1,4,128]{3,0,2,1:T(8,128)(2,1)S(1)}, u32[]{:S(2)}, u32[]{:S(2)}) collective-permute-start(bf16[64,1,4,128]{3,0,2,1:T(8,128)(2,1)S(1)} %bitcast.189), channel_id=1, source_target_pairs={{0,7},{1,0},{2,1},{3,2},{4,3},{5,4},{6,5},{7,6},{8,15},{9,8},{10,9... | collective-permute-start | bytes 196616 | tf_op jit(solution)/shard_map/ppermute | solution.py:118
  85.2 6.8 %collective-permute-start.3 = (bf16[64,1,4,128]{3,0,2,1:T(8,128)(2,1)S(1)}, bf16[64,1,4,128]{3,0,2,1:T(8,128)(2,1)S(1)}, u32[]{:S(2)}, u32[]{:S(2)}) collective-permute-start(bf16[64,1,4,128]{3,0,2,1:T(8,128)(2,1)S(1)} %collective-permute-done.1), channel_id=1, source_target_pairs={{0,1},{1,2},{2,3},{3,4},{4,5},{5,6},{6,7},{7,0},{8,9},{9,10},{10,1... | collective-permute-start | bytes 196616 | tf_op jit(solution)/shard_map/ppermute | solution.py:116
  87.2 7.0 %collective-permute-start.2 = (bf16[64,1,4,128]{3,0,2,1:T(8,128)(2,1)S(1)}, bf16[64,1,4,128]{3,0,2,1:T(8,128)(2,1)S(1)}, u32[]{:S(2)}, u32[]{:S(2)}) collective-permute-start(bf16[64,1,4,128]{3,0,2,1:T(8,128)(2,1)S(1)} %collective-permute-done), channel_id=1, source_target_pairs={{0,7},{1,0},{2,1},{3,2},{4,3},{5,4},{6,5},{7,6},{8,15},{9,8},{10,9... | collective-permute-start | bytes 196616 | tf_op jit(solution)/shard_map/ppermute | solution.py:118
  92.1 6.8 %collective-permute-start.5 = (bf16[64,1,4,128]{3,0,2,1:T(8,128)(2,1)S(1)}, bf16[64,1,4,128]{3,0,2,1:T(8,128)(2,1)S(1)}, u32[]{:S(2)}, u32[]{:S(2)}) collective-permute-start(bf16[64,1,4,128]{3,0,2,1:T(8,128)(2,1)S(1)} %collective-permute-done.3), channel_id=1, source_target_pairs={{0,1},{1,2},{2,3},{3,4},{4,5},{5,6},{6,7},{7,0},{8,9},{9,10},{10,1... | collective-permute-start | bytes 196616 | tf_op jit(solution)/shard_map/ppermute | solution.py:116
  94.2 6.8 %collective-permute-start.4 = (bf16[64,1,4,128]{3,0,2,1:T(8,128)(2,1)S(1)}, bf16[64,1,4,128]{3,0,2,1:T(8,128)(2,1)S(1)}, u32[]{:S(2)}, u32[]{:S(2)}) collective-permute-start(bf16[64,1,4,128]{3,0,2,1:T(8,128)(2,1)S(1)} %collective-permute-done.2), channel_id=1, source_target_pairs={{0,7},{1,0},{2,1},{3,2},{4,3},{5,4},{6,5},{7,6},{8,15},{9,8},{10,9... | collective-permute-start | bytes 196616 | tf_op jit(solution)/shard_map/ppermute | solution.py:118
  98.9 6.2 %collective-permute-start.6 = (bf16[64,1,4,128]{3,0,2,1:T(8,128)(2,1)S(1)}, bf16[64,1,4,128]{3,0,2,1:T(8,128)(2,1)S(1)}, u32[]{:S(2)}, u32[]{:S(2)}) collective-permute-start(bf16[64,1,4,128]{3,0,2,1:T(8,128)(2,1)S(1)} %collective-permute-done.5), channel_id=1, source_target_pairs={{0,1},{1,2},{2,3},{3,4},{4,5},{5,6},{6,7},{7,0},{8,9},{9,10},{10,1... | collective-permute-start | bytes 196616 | tf_op jit(solution)/shard_map/ppermute | solution.py:116
  106.0 21.0 %all-to-all-start.1 = ((bf16[64,1,4,128]{3,2,1,0:T(4,128)(2,1)}), bf16[64,1,4,128]{3,2,1,0:T(4,128)(2,1)S(1)}, u32[]{:S(2)}, u32[]{:S(2)}) async-start(bf16[64,1,4,128]{3,2,1,0:T(4,128)(2,1)} %copy.46), calls=%async_computation.1 | async-start | bytes 131072 | tf_op jit(solution)/shard_map/all_to_all | solution.py:49
